TPU v7x, 512 devices: a whole 4x8x8 slice. The times are simulated.
512 devices in a mesh: layer: 16 (over x, z_hi, core), col: 32 (over z_lo, y).
Axes of the slice: x: 4, y: 8, z: 8 (z_hi: 2, z_lo: 4; z = z_hi * 4 + z_lo), core: 2. Of those that a mesh axis runs over, the one named last changes fastest.
Arguments:
- lower_panel: bfloat16 [16, 4096, 768], P('layer', 'col'), may hold values from -0.109375 to 0.109375
- upper_panel: bfloat16 [16, 768, 4096], P('layer', None, 'col'), may hold values from -6 to 6
- diag_inverse: bfloat16 [16, 1, 768, 768], P('layer'), may hold values from -1 to 2, as said below
- pivot_inverse: bfloat16 [4, 128, 128], replicated, may hold values from -0.1 to 0.1, as said below
- pattern: int32 [16, 2, 32], P('layer'), may hold values 0 or 1
- col_order: int32 [32], replicated, may hold values from 0 to 31, each once
- sep_blocks: int32 [4], replicated, may hold values from 0 to 31, as said below
Outputs:
- schur_top: bfloat16 [4096, 4096], P('layer', 'col')
Inputs may be any that keep to these rules, and one draw needn't show every extreme that they name: `diag_inverse`: each is the identity plus a full matrix of smaller entries. `pivot_inverse`: full matrices. `sep_blocks`: the 4 entries are distinct.
All inputs are finite; a program needn't handle non-finite values. No bound on the sum of `pattern` on one device may be relied on, other than what follows from the above.
Results may differ from a plain program's by a relative error of at most 0.0088.
Values may be sent and summed in bfloat16 or wider, within the bound.
No kernel may reach another device: no remote copies, remote signals or barrier semaphores. Data moves between devices by JAX's collectives and lax.ppermute only.
A program may use at most 64 MiB of HBM per device.

v0:
```python
import jax
import jax.numpy as jnp
from jax import lax
from jax.experimental import pallas as pl
from jax.experimental.pallas import tpu as pltpu
from jax.sharding import Mesh
from jax.sharding import PartitionSpec as P

NB = 128
COL = ("zl", "y")
F32 = jnp.float32
BF16 = jnp.bfloat16


def dot(a, b):
    return jnp.dot(a, b, preferred_element_type=F32)


def swap(value, axis, mask):
    return lax.ppermute(value, axis, [(i, i ^ mask) for i in range(lax.axis_size(axis))])


def spread(value, axis, n):
    return lax.all_to_all(jnp.broadcast_to(value[None], (n,) + value.shape), axis, 0, 0, tiled=True)


VMEM = pl.BlockSpec(memory_space=pltpu.VMEM)
SMEM = pl.BlockSpec(memory_space=pltpu.SMEM)


def solve_into(diag_ref, upper, scale, out_ref, columns):
    supernodes, node = diag_ref.shape[0], diag_ref.shape[1]
    for s in range(supernodes):
        here = pl.ds(s * node, node)
        solved = dot(diag_ref[s], upper[s * node : (s + 1) * node])
        out_ref[here, columns] = (solved * scale).astype(BF16)


def sep_kernel(col_ref, row_ref, parts_ref, diag_ref, upper_ref, pos_ref, own_ref, state_ref, left_ref):
    levels = row_ref.shape[0]
    wide = levels * NB
    lane = lax.broadcasted_iota(jnp.int32, (1, 2 * NB), 1)
    solve_into(diag_ref, upper_ref[...], col_ref[levels], own_ref, pl.ds(0, NB))
    for k in range(0, levels, 2):
        upper = jnp.concatenate([parts_ref[levels + k], parts_ref[levels + k + 1]], axis=1)
        scale = jnp.where(lane < NB, col_ref[k], col_ref[k + 1])
        solve_into(diag_ref, upper, scale, pos_ref, pl.ds(k * NB, 2 * NB))
    for k in range(levels):
        for j in range(left_ref.shape[1] // NB):
            left_ref[k * NB : (k + 1) * NB, j * NB : (j + 1) * NB] = parts_ref[k, j * NB : (j + 1) * NB, :]
    low = lax.broadcasted_iota(jnp.int32, (wide, 1), 0) // NB
    sign = jnp.zeros((wide, 1), F32)
    for k in range(levels):
        sign = jnp.where(low == k, -row_ref[k], sign)
    state_ref[:, :wide] = (dot(left_ref[...], pos_ref[...]) * sign).astype(BF16)
    state_ref[:, wide:] = (dot(left_ref[...], own_ref[...]) * sign).astype(BF16)


def product_kernel(pick_ref, flag_ref, left_ref, *refs):
    out_ref, right_ref = refs[-2:]
    for r, part in enumerate(refs[:-2]):
        right_ref[r] = part[...]
    right = jnp.concatenate([right_ref[pick_ref[0]], right_ref[pick_ref[1]]], axis=1)
    for q in range(left_ref.shape[0]):
        here = pl.ds(q * NB, NB)
        out_ref[here, :] = (dot(left_ref[q], right) * flag_ref[q]).astype(out_ref.dtype)


def call(kernel, outs, specs, scratch=(), dtype=BF16):
    return pl.pallas_call(
        kernel,
        out_shape=[jax.ShapeDtypeStruct(o, dtype) for o in outs],
        in_specs=specs,
        out_specs=[VMEM] * len(outs),
        scratch_shapes=list(scratch),
        compiler_params=pltpu.CompilerParams(vmem_limit_bytes=40 * 2**20),
    )


def shards(lower_panel, upper_panel, diag_inverse, pivot_inverse, pattern, col_order, sep_blocks):
    width = diag_inverse.shape[1] * diag_inverse.shape[2]
    nz, ny = lax.axis_size("zl"), lax.axis_size("y")
    zl, y, x = lax.axis_index("zl"), lax.axis_index("y"), lax.axis_index("x")
    zh, core = lax.axis_index("zh"), lax.axis_index("core")
    ncol = nz * ny
    me = zl * ny + y
    layer = (x * 2 + zh) * 2 + core
    levels = sep_blocks.shape[0]
    nblocks = col_order.shape[0]
    positions = jnp.arange(nblocks, dtype=jnp.int32)
    pos_blocks = jnp.sum(jnp.where(col_order[None, :] == sep_blocks[:, None], positions[None, :], 0), axis=1)
    row_flags, col_flags = pattern[0, 0].astype(F32), pattern[0, 1].astype(F32)
    left, upper_own = lower_panel[0], upper_panel[0]

    kblocks = width // NB
    rows = width // ncol
    left_stack = left.reshape(NB, kblocks, NB).transpose(1, 0, 2).reshape(ncol, rows, NB)
    send = jnp.stack([left_stack, upper_own.reshape(ncol, rows, NB)], axis=1)
    got = lax.all_to_all(send, COL, 0, 0, tiled=True)
    picked = [lax.dynamic_index_in_dim(got[:, 0], sep_blocks[k], 0) for k in range(levels)]
    picked += [lax.dynamic_index_in_dim(got[:, 1], pos_blocks[k], 0) for k in range(levels)]
    picked = jnp.concatenate(picked, 0)
    picked, left_late = lax.optimization_barrier((picked, left))
    parts = spread(picked, COL, ncol).transpose(1, 0, 2, 3).reshape(2 * levels, width, NB)
    left_moved = lax.ppermute(
        left_late, COL, [(a * ny + b, (b // 2) * ny + 2 * a + b % 2) for a in range(nz) for b in range(ny)]
    )

    pos_width, half = levels * NB, nz * NB // 2
    flags = jnp.concatenate([col_flags[pos_blocks], col_flags[me][None]])
    right_pos, right_own, state = call(
        sep_kernel,
        [(width, pos_width), (width, NB), (pos_width, pos_width + NB)],
        [SMEM] * 2 + [VMEM] * 3,
        [pltpu.VMEM((pos_width, width), BF16)],
    )(flags, row_flags[sep_blocks], parts, diag_inverse[0], upper_own)

    state, left_moved = lax.optimization_barrier((state, left_moved))
    left_tile = spread(left_moved, "y", ny)
    panels, fills = [], []
    axes = (("core", 1), ("zh", 1), ("x", 1), ("x", 2))
    for k in range(levels):
        if k == levels - 1:
            state = state[:, NB:]
        axis, mask = axes[k]
        other = swap(state, axis, mask)
        total = state.astype(F32) + other.astype(F32)
        skip = NB if k < levels - 1 else 0
        fill = dot(pivot_inverse[k], total[:NB, skip:].astype(BF16)).astype(BF16)
        if k < levels - 1:
            panel = total[NB:, :NB].astype(BF16)
            state = (total[NB:, NB:] - dot(panel, fill)).astype(BF16)
        fills.append(fill)
        own = right_pos[:, k * NB : (k + 1) * NB]
        if k:
            before = jnp.concatenate([fills[m][:, (k - m - 1) * NB : (k - m) * NB] for m in range(k)], axis=0)
            own = (own.astype(F32) - dot(jnp.concatenate(panels, axis=1), before)).astype(BF16)
        panels.append(own)
    fill_own = jnp.concatenate([f[:, -NB:] for f in fills], axis=0)
    right_new = (right_own.astype(F32) - dot(jnp.concatenate(panels, axis=1), fill_own)).astype(BF16)
    right_parts = [right_new] + [
        lax.ppermute(right_new, "zl", [(i, (i + r) % nz) for i in range(nz)]) for r in range(1, nz)
    ]

    tile_rows = jnp.arange(nz, dtype=jnp.int32)[:, None] * 8 + 2 * zl + jnp.arange(2, dtype=jnp.int32)[None, :]
    tile_flags = -row_flags[tile_rows.reshape(-1)]

    def product(which, dtype):
        picks = (zl - 2 * which - jnp.arange(2, dtype=jnp.int32)) % nz
        specs = [SMEM] * 2 + [VMEM] * (1 + nz)
        scratch = [pltpu.VMEM((nz, width, NB), BF16)]
        return call(product_kernel, [(ny * NB, half)], specs, scratch, dtype)(picks, tile_flags, left_tile, *right_parts)[0]

    taken = swap(product(1 - core, BF16), "core", 1)
    both = (product(core, F32) + taken.astype(F32)).astype(BF16).reshape(nz, 2 * NB, half)
    summed = jnp.sum(lax.all_to_all(both, "x", 0, 0, tiled=True).astype(F32), axis=0)
    pairs = [
        [((a * 2 + b) * nz + c, c * nz + 2 * b + (r ^ a)) for a in range(2) for b in range(2) for c in range(nz)]
        for r in range(2)
    ]
    summed = summed.astype(BF16)
    first = lax.dynamic_slice_in_dim(summed, zh * NB, NB, 1)
    second = lax.dynamic_slice_in_dim(summed, (1 - zh) * NB, NB, 1)
    first = lax.ppermute(first, ("zh", "core", "zl"), pairs[0])
    second = lax.ppermute(second, ("zh", "core", "zl"), pairs[1])
    out = first.astype(F32) + second.astype(F32)
    row_blocks = layer * 2 + jnp.arange(2 * NB, dtype=jnp.int32) // NB
    row_keep = jnp.all(row_blocks[:, None] != sep_blocks[None, :], axis=1)
    col_keep = jnp.all(pos_blocks != me)
    return jnp.where(row_keep[:, None] & col_keep, out, 0.0).astype(BF16)


def solution(mesh):
    fine = Mesh(mesh.devices.reshape(4, 2, 2, 4, 8), ("x", "zh", "core", "zl", "y"))
    lay = ("x", "zh", "core")
    in_specs = (
        P(lay, COL, None),
        P(lay, None, COL),
        P(lay, None, None, None),
        P(),
        P(lay, None, None),
        P(),
        P(),
    )
    return jax.shard_map(shards, mesh=fine, in_specs=in_specs, out_specs=P(lay, COL), check_vma=False)
```

profile of v0, /device:TPU:64, one launch (start us, length us, event | category | flops | bytes accessed | tf_op | source)
XLA Modules:
  0.0 203.2 jit_solution(8612274158053770129)
XLA Ops:
  0.0 1.1 copy.26
  1.3 1.0 pad_maximum_fusion
  2.3 0.8 copy.28
  3.1 12.3 %all-to-all-start = ((bf16[32,2,24,128]{3,2,1,0:T(8,128)(2,1)}), bf16[32,2,24,128]{3,2,1,0:T(8,128)(2,1)S(1)}, u32[]{:S(2)}, u32[]{:S(2)}) async-start(bf16[32,2,24,128]{3,2,1,0:T(8,128)(2,1)} %copy.28), calls=%async_computation | async-start | bytes 786432 | tf_op jit(solution)/shard_map/all_to_all | solution.py:99
  15.4 0.6 fusion.78
  21.2 0.7 fusion.77
  32.2 1.5 broadcast_in_dim.30
  33.8 10.3 %all-to-all-start.1 = ((bf16[32,8,24,128]{3,2,1,0:T(8,128)(2,1)}), bf16[32,8,24,128]{3,2,1,0:T(8,128)(2,1)S(1)}, u32[]{:S(2)}, u32[]{:S(2)}) async-start(bf16[32,8,24,128]{3,2,1,0:T(8,128)(2,1)} %broadcast_in_dim.30), calls=%async_computation.1 | async-start | bytes 3145728 | tf_op jit(solution)/shard_map/all_to_all | solution.py:24
  44.2 0.6 constant_dynamic-slice_fusion.2
  44.8 0.6 gather_fusion.1
  45.5 4.3 %collective-permute-start = (bf16[128,768]{1,0:T(8,128)(2,1)}, bf16[128,768]{1,0:T(8,128)(2,1)S(1)}, u32[]{:S(2)}, u32[]{:S(2)}) collective-permute-start(bf16[128,768]{1,0:T(8,128)(2,1)} %bitcast.26), channel_id=1, source_target_pairs={{0,0},{1,1},{2,8},{3,9},{4,16},{5,17},{6,24},{7,25},{8,2},{9,3},{1... | collective-permute-start | bytes 589832 | tf_op jit(solution)/shard_map/ppermute | solution.py:105
  49.8 0.6 gather_fusion.2
  50.4 0.7 pad_maximum_fusion.1.col_ref
  51.1 32.3 %all-to-all-done.1 = bf16[32,8,24,128]{3,2,1,0:T(8,128)(2,1)S(1)} async-done(((bf16[32,8,24,128]{3,2,1,0:T(8,128)(2,1)}), bf16[32,8,24,128]{3,2,1,0:T(8,128)(2,1)S(1)}, u32[]{:S(2)}, u32[]{:S(2)}) %all-to-all-start.1) | async-done | bytes 1572896 | tf_op jit(solution)/shard_map/all_to_all | solution.py:24
  83.7 1.0 copy-done
  84.7 2.3 %shard_map.73 = (bf16[768,512]{1,0:T(8,128)(2,1)S(1)}, bf16[768,128]{1,0:T(8,128)(2,1)S(1)}, bf16[512,640]{1,0:T(8,128)(2,1)S(1)}) custom-call(f32[5]{0:T(128)S(1)} %pad_maximum_fusion.1.col_ref, f32[4]{0:T(128)S(1)} %gather_fusion.2, bf16[8,768,128]{2,1,0:T(8,128)(2,1)S(1)} %bitcast.66, bf16[1,768,768]{2,1,0:T(8,128)(2,1)S(1)} %bitcast.67, ...), custom_call_target="tpu_custom_call" | custom-call | tf_op jit(solution)/shard_map/pallas_call | solution.py:111
  87.0 5.8 %collective-permute-done = bf16[128,768]{1,0:T(8,128)(2,1)S(1)} collective-permute-done((bf16[128,768]{1,0:T(8,128)(2,1)}, bf16[128,768]{1,0:T(8,128)(2,1)S(1)}, u32[]{:S(2)}, u32[]{:S(2)}) %collective-permute-start) | collective-permute-done | bytes 196640 | tf_op jit(solution)/shard_map/ppermute | solution.py:105
  92.8 1.9 collective-permute-start.1
  94.7 0.7 slice.141
  95.4 1.3 broadcast_in_dim.54
  96.7 7.9 %all-to-all-start.2 = ((bf16[8,128,768]{2,1,0:T(8,128)(2,1)}), bf16[8,128,768]{2,1,0:T(8,128)(2,1)S(1)}, u32[]{:S(2)}, u32[]{:S(2)}) async-start(bf16[8,128,768]{2,1,0:T(8,128)(2,1)} %broadcast_in_dim.54), calls=%async_computation.2 | async-start | bytes 3145728 | tf_op jit(solution)/shard_map/all_to_all | solution.py:24
  104.7 1.3 convert_add_fusion
  106.4 8.2 %collective-permute-start.2 = (bf16[384,512]{1,0:T(8,128)(2,1)S(1)}, bf16[384,512]{1,0:T(8,128)(2,1)S(1)}, u32[]{:S(2)}, u32[]{:S(2)}) collective-permute-start(bf16[384,512]{1,0:T(8,128)(2,1)S(1)} %fusion.5), channel_id=1, source_target_pairs={{0,64},{64,0},{1,65},{65,1},{2,66},{66,2},{3,67},{67,3},{4,68},{68... | collective-permute-start | bytes 1179656 | tf_op jit(solution)/shard_map/ppermute | solution.py:20
  114.9 17.4 %collective-permute-done.2 = bf16[384,512]{1,0:T(8,128)(2,1)S(1)} collective-permute-done((bf16[384,512]{1,0:T(8,128)(2,1)S(1)}, bf16[384,512]{1,0:T(8,128)(2,1)S(1)}, u32[]{:S(2)}, u32[]{:S(2)}) %collective-permute-start.2) | collective-permute-done | bytes 393248 | tf_op jit(solution)/shard_map/ppermute | solution.py:20
  132.8 3.4 %collective-permute-start.3 = (bf16[256,384]{1,0:T(8,128)(2,1)S(1)}, bf16[256,384]{1,0:T(8,128)(2,1)S(1)}, u32[]{:S(2)}, u32[]{:S(2)}) collective-permute-start(bf16[256,384]{1,0:T(8,128)(2,1)S(1)} %fusion.18), channel_id=1, source_target_pairs={{0,128},{128,0},{256,384},{384,256},{1,129},{129,1},{257,385},{385... | collective-permute-start | bytes 589832 | tf_op jit(solution)/shard_map/ppermute | solution.py:20
  136.5 4.9 %collective-permute-done.3 = bf16[256,384]{1,0:T(8,128)(2,1)S(1)} collective-permute-done((bf16[256,384]{1,0:T(8,128)(2,1)S(1)}, bf16[256,384]{1,0:T(8,128)(2,1)S(1)}, u32[]{:S(2)}, u32[]{:S(2)}) %collective-permute-start.3) | collective-permute-done | bytes 196640 | tf_op jit(solution)/shard_map/ppermute | solution.py:20
  141.8 4.9 %collective-permute-start.4 = (bf16[128,128]{1,0:T(8,128)(2,1)S(1)}, bf16[128,128]{1,0:T(8,128)(2,1)S(1)}, u32[]{:S(2)}, u32[]{:S(2)}) collective-permute-start(bf16[128,128]{1,0:T(8,128)(2,1)S(1)} %fusion.40), channel_id=1, source_target_pairs={{0,256},{128,384},{256,0},{384,128},{1,257},{129,385},{257,1},{385... | collective-permute-start | bytes 98312 | tf_op jit(solution)/shard_map/ppermute | solution.py:20
  147.1 2.0 collective-permute-done.4
  149.7 1.9 collective-permute-start.5
  151.6 5.4 %collective-permute-start.6 = (bf16[768,128]{1,0:T(8,128)(2,1)S(1)}, bf16[768,128]{1,0:T(8,128)(2,1)S(1)}, u32[]{:S(2)}, u32[]{:S(2)}) collective-permute-start(bf16[768,128]{1,0:T(8,128)(2,1)S(1)} %fusion.refs_0_), channel_id=1, source_target_pairs={{0,16},{8,24},{16,0},{24,8},{1,17},{9,25},{17,1},{25,9},{2,18},{10... | collective-permute-start | bytes 589832 | tf_op jit(solution)/shard_map/ppermute | solution.py:142
  157.0 1.9 collective-permute-start.7
  158.9 0.6 gather_fusion
  159.6 4.9 %collective-permute-done.5.refs_1_ = bf16[768,128]{1,0:T(8,128)(2,1)S(1)} collective-permute-done((bf16[768,128]{1,0:T(8,128)(2,1)S(1)}, bf16[768,128]{1,0:T(8,128)(2,1)S(1)}, u32[]{:S(2)}, u32[]{:S(2)}) %collective-permute-start.5) | collective-permute-done | bytes 196640 | tf_op jit(solution)/shard_map/ppermute | solution.py:142
  164.5 2.9 %collective-permute-done.6.refs_2_ = bf16[768,128]{1,0:T(8,128)(2,1)S(1)} collective-permute-done((bf16[768,128]{1,0:T(8,128)(2,1)S(1)}, bf16[768,128]{1,0:T(8,128)(2,1)S(1)}, u32[]{:S(2)}, u32[]{:S(2)}) %collective-permute-start.6) | collective-permute-done | bytes 196640 | tf_op jit(solution)/shard_map/ppermute | solution.py:142
  167.4 2.7 %collective-permute-done.7.refs_3_ = bf16[768,128]{1,0:T(8,128)(2,1)S(1)} collective-permute-done((bf16[768,128]{1,0:T(8,128)(2,1)S(1)}, bf16[768,128]{1,0:T(8,128)(2,1)S(1)}, u32[]{:S(2)}, u32[]{:S(2)}) %collective-permute-start.7) | collective-permute-done | bytes 196640 | tf_op jit(solution)/shard_map/ppermute | solution.py:142
  170.1 1.2 shard_map.75
  171.3 1.9 collective-permute-start.8
  173.3 1.2 shard_map.74
  174.4 0.7 collective-permute-done.8
  175.1 0.9 add_convert_fusion
  176.1 4.3 %all-to-all-start.3 = ((bf16[4,256,256]{2,1,0:T(8,128)(2,1)}), bf16[4,256,256]{2,1,0:T(8,128)(2,1)S(1)}, u32[]{:S(2)}, u32[]{:S(2)}) async-start(bf16[4,256,256]{2,1,0:T(8,128)(2,1)} %bitcast.39), calls=%async_computation.3 | async-start | bytes 1048576 | tf_op jit(solution)/shard_map/all_to_all | solution.py:156
  180.4 0.6 compare_reduce_fusion.1
  181.1 9.1 %all-to-all-done.3 = bf16[4,256,256]{2,1,0:T(8,128)(2,1)S(1)} async-done(((bf16[4,256,256]{2,1,0:T(8,128)(2,1)}), bf16[4,256,256]{2,1,0:T(8,128)(2,1)S(1)}, u32[]{:S(2)}, u32[]{:S(2)}) %all-to-all-start.3) | async-done | bytes 524320 | tf_op jit(solution)/shard_map/all_to_all | solution.py:156
  190.3 1.9 collective-permute-start.10
  192.2 3.7 %collective-permute-start.9 = (bf16[256,128]{1,0:T(8,128)(2,1)S(1)}, bf16[256,128]{1,0:T(8,128)(2,1)S(1)}, u32[]{:S(2)}, u32[]{:S(2)}) collective-permute-start(bf16[256,128]{1,0:T(8,128)(2,1)S(1)} %get-tuple-element.27), channel_id=1, source_target_pairs={{0,0},{8,32},{16,64},{24,96},{32,16},{40,48},{48,80},{56,112},{64,... | collective-permute-start | bytes 196616 | tf_op jit(solution)/shard_map/ppermute | solution.py:164
  195.9 0.7 broadcast_and_fusion
  196.6 5.8 %collective-permute-done.9 = bf16[256,128]{1,0:T(8,128)(2,1)S(1)} collective-permute-done((bf16[256,128]{1,0:T(8,128)(2,1)S(1)}, bf16[256,128]{1,0:T(8,128)(2,1)S(1)}, u32[]{:S(2)}, u32[]{:S(2)}) %collective-permute-start.9) | collective-permute-done | bytes 65568 | tf_op jit(solution)/shard_map/ppermute | solution.py:164
  202.5 0.7 select_convert_fusion
  (63 shorter events, 3.9 us)
Async XLA Ops:
  0.0 15.4 %copy-start.4 = (s32[4]{0:T(128)S(1)}, s32[4]{0:T(128)}, u32[]{:S(2)}) copy-start(s32[4]{0:T(128)} %param.13) | copy-start | bytes 52
  0.0 21.0 %copy-start.6 = (s32[32]{0:T(128)S(1)}, s32[32]{0:T(128)}, u32[]{:S(2)}) copy-start(s32[32]{0:T(128)} %param.12) | copy-start | bytes 388
  3.1 29.0 %all-to-all-start = ((bf16[32,2,24,128]{3,2,1,0:T(8,128)(2,1)}), bf16[32,2,24,128]{3,2,1,0:T(8,128)(2,1)S(1)}, u32[]{:S(2)}, u32[]{:S(2)}) async-start(bf16[32,2,24,128]{3,2,1,0:T(8,128)(2,1)} %copy.28), calls=%async_computation | async-start | bytes 786432 | tf_op jit(solution)/shard_map/all_to_all | solution.py:99
  33.8 10.5 %copy-start.5 = (s32[1,2,32]{2,1,0:T(2,128)S(1)}, s32[1,2,32]{2,1,0:T(2,128)}, u32[]{:S(2)}) copy-start(s32[1,2,32]{2,1,0:T(2,128)} %param.11) | copy-start | bytes 772
  33.8 49.7 %all-to-all-start.1 = ((bf16[32,8,24,128]{3,2,1,0:T(8,128)(2,1)}), bf16[32,8,24,128]{3,2,1,0:T(8,128)(2,1)S(1)}, u32[]{:S(2)}, u32[]{:S(2)}) async-start(bf16[32,8,24,128]{3,2,1,0:T(8,128)(2,1)} %broadcast_in_dim.30), calls=%async_computation.1 | async-start | bytes 3145728 | tf_op jit(solution)/shard_map/all_to_all | solution.py:24
  45.5 47.3 %collective-permute-start = (bf16[128,768]{1,0:T(8,128)(2,1)}, bf16[128,768]{1,0:T(8,128)(2,1)S(1)}, u32[]{:S(2)}, u32[]{:S(2)}) collective-permute-start(bf16[128,768]{1,0:T(8,128)(2,1)} %bitcast.26), channel_id=1, source_target_pairs={{0,0},{1,1},{2,8},{3,9},{4,16},{5,17},{6,24},{7,25},{8,2},{9,3},{1... | collective-permute-start | bytes 589832 | tf_op jit(solution)/shard_map/ppermute | solution.py:105
  83.4 1.3 copy-start
  83.4 1.3 copy-start.1
  92.8 11.9 %collective-permute-start.1 = (bf16[512,640]{1,0:T(8,128)(2,1)S(1)}, bf16[512,640]{1,0:T(8,128)(2,1)}, u32[]{:S(2)}, u32[]{:S(2)}) collective-permute-start(bf16[512,640]{1,0:T(8,128)(2,1)S(1)} %get-tuple-element.18), channel_id=1, source_target_pairs={{0,32},{32,0},{1,33},{33,1},{2,34},{34,2},{3,35},{35,3},{4,36},{36... | collective-permute-start | bytes 1966088 | tf_op jit(solution)/shard_map/ppermute | solution.py:20
  96.7 73.4 %all-to-all-start.2 = ((bf16[8,128,768]{2,1,0:T(8,128)(2,1)}), bf16[8,128,768]{2,1,0:T(8,128)(2,1)S(1)}, u32[]{:S(2)}, u32[]{:S(2)}) async-start(bf16[8,128,768]{2,1,0:T(8,128)(2,1)} %broadcast_in_dim.54), calls=%async_computation.2 | async-start | bytes 3145728 | tf_op jit(solution)/shard_map/all_to_all | solution.py:24
  104.6 1.3 copy-start.3
  106.4 25.9 %collective-permute-start.2 = (bf16[384,512]{1,0:T(8,128)(2,1)S(1)}, bf16[384,512]{1,0:T(8,128)(2,1)S(1)}, u32[]{:S(2)}, u32[]{:S(2)}) collective-permute-start(bf16[384,512]{1,0:T(8,128)(2,1)S(1)} %fusion.5), channel_id=1, source_target_pairs={{0,64},{64,0},{1,65},{65,1},{2,66},{66,2},{3,67},{67,3},{4,68},{68... | collective-permute-start | bytes 1179656 | tf_op jit(solution)/shard_map/ppermute | solution.py:20
  114.9 21.4 %copy-start.2 = (bf16[768,128]{1,0:T(8,128)(2,1)S(1)}, bf16[768,128]{1,0:T(8,128)(2,1)}, u32[]{:S(2)}) copy-start(bf16[768,128]{1,0:T(8,128)(2,1)} %slice.141) | copy-start | bytes 589828
  132.8 8.7 %collective-permute-start.3 = (bf16[256,384]{1,0:T(8,128)(2,1)S(1)}, bf16[256,384]{1,0:T(8,128)(2,1)S(1)}, u32[]{:S(2)}, u32[]{:S(2)}) collective-permute-start(bf16[256,384]{1,0:T(8,128)(2,1)S(1)} %fusion.18), channel_id=1, source_target_pairs={{0,128},{128,0},{256,384},{384,256},{1,129},{129,1},{257,385},{385... | collective-permute-start | bytes 589832 | tf_op jit(solution)/shard_map/ppermute | solution.py:20
  141.8 7.3 %collective-permute-start.4 = (bf16[128,128]{1,0:T(8,128)(2,1)S(1)}, bf16[128,128]{1,0:T(8,128)(2,1)S(1)}, u32[]{:S(2)}, u32[]{:S(2)}) collective-permute-start(bf16[128,128]{1,0:T(8,128)(2,1)S(1)} %fusion.40), channel_id=1, source_target_pairs={{0,256},{128,384},{256,0},{384,128},{1,257},{129,385},{257,1},{385... | collective-permute-start | bytes 98312 | tf_op jit(solution)/shard_map/ppermute | solution.py:20
  149.7 14.8 %collective-permute-start.5 = (bf16[768,128]{1,0:T(8,128)(2,1)S(1)}, bf16[768,128]{1,0:T(8,128)(2,1)S(1)}, u32[]{:S(2)}, u32[]{:S(2)}) collective-permute-start(bf16[768,128]{1,0:T(8,128)(2,1)S(1)} %fusion.refs_0_), channel_id=1, source_target_pairs={{0,8},{8,16},{16,24},{24,0},{1,9},{9,17},{17,25},{25,1},{2,10},{10... | collective-permute-start | bytes 589832 | tf_op jit(solution)/shard_map/ppermute | solution.py:142
  151.6 15.8 %collective-permute-start.6 = (bf16[768,128]{1,0:T(8,128)(2,1)S(1)}, bf16[768,128]{1,0:T(8,128)(2,1)S(1)}, u32[]{:S(2)}, u32[]{:S(2)}) collective-permute-start(bf16[768,128]{1,0:T(8,128)(2,1)S(1)} %fusion.refs_0_), channel_id=1, source_target_pairs={{0,16},{8,24},{16,0},{24,8},{1,17},{9,25},{17,1},{25,9},{2,18},{10... | collective-permute-start | bytes 589832 | tf_op jit(solution)/shard_map/ppermute | solution.py:142
  157.0 13.2 %collective-permute-start.7 = (bf16[768,128]{1,0:T(8,128)(2,1)S(1)}, bf16[768,128]{1,0:T(8,128)(2,1)S(1)}, u32[]{:S(2)}, u32[]{:S(2)}) collective-permute-start(bf16[768,128]{1,0:T(8,128)(2,1)S(1)} %fusion.refs_0_), channel_id=1, source_target_pairs={{0,24},{8,0},{16,8},{24,16},{1,25},{9,1},{17,9},{25,17},{2,26},{10... | collective-permute-start | bytes 589832 | tf_op jit(solution)/shard_map/ppermute | solution.py:142
  171.3 3.8 %collective-permute-start.8 = (bf16[1024,256]{1,0:T(8,128)(2,1)S(1)}, bf16[1024,256]{1,0:T(8,128)(2,1)S(1)}, u32[]{:S(2)}, u32[]{:S(2)}) collective-permute-start(bf16[1024,256]{1,0:T(8,128)(2,1)S(1)} %shard_map.75), channel_id=1, source_target_pairs={{0,32},{32,0},{1,33},{33,1},{2,34},{34,2},{3,35},{35,3},{4,36},{36... | collective-permute-start | bytes 1572872 | tf_op jit(solution)/shard_map/ppermute | solution.py:20
  176.1 14.1 %all-to-all-start.3 = ((bf16[4,256,256]{2,1,0:T(8,128)(2,1)}), bf16[4,256,256]{2,1,0:T(8,128)(2,1)S(1)}, u32[]{:S(2)}, u32[]{:S(2)}) async-start(bf16[4,256,256]{2,1,0:T(8,128)(2,1)} %bitcast.39), calls=%async_computation.3 | async-start | bytes 1048576 | tf_op jit(solution)/shard_map/all_to_all | solution.py:156
  190.3 6.4 %collective-permute-start.10 = (bf16[256,128]{1,0:T(8,128)(2,1)S(1)}, bf16[256,128]{1,0:T(8,128)(2,1)S(1)}, u32[]{:S(2)}, u32[]{:S(2)}) collective-permute-start(bf16[256,128]{1,0:T(8,128)(2,1)S(1)} %get-tuple-element.28), channel_id=1, source_target_pairs={{0,8},{8,40},{16,72},{24,104},{32,24},{40,56},{48,88},{56,120},{64... | collective-permute-start | bytes 196616 | tf_op jit(solution)/shard_map/ppermute | solution.py:165
  192.2 10.3 %collective-permute-start.9 = (bf16[256,128]{1,0:T(8,128)(2,1)S(1)}, bf16[256,128]{1,0:T(8,128)(2,1)S(1)}, u32[]{:S(2)}, u32[]{:S(2)}) collective-permute-start(bf16[256,128]{1,0:T(8,128)(2,1)S(1)} %get-tuple-element.27), channel_id=1, source_target_pairs={{0,0},{8,32},{16,64},{24,96},{32,16},{40,48},{48,80},{56,112},{64,... | collective-permute-start | bytes 196616 | tf_op jit(solution)/shard_map/ppermute | solution.py:164
where the time goes:
time: 204 us; the launch traced here: 203 us
  waiting for transfers between devices  88.6 us (43%)
  starting transfers between devices  74.4 us (36%)
  between operations  15.5 us (8%)
  local copies, waits for them, and re-layouts  11 us (5%)
  other arithmetic  6.65 us (3%)
  Pallas kernels  4.63 us (2%)
  matrix products  2.33 us (1%)
    all_to_all x2, waiting for transfers between devices, spread(): lax.all_to_all(jnp.broadcast_to(value[None], (n,) + value.shape), axis, 0...  32.3 us
    ppermute x5, waiting for transfers between devices, swap(): lax.ppermute(value, axis, [(i, i ^ mask) for i in range(lax.axis_size(axi...  25 us
    ppermute x5, starting transfers between devices, swap(): lax.ppermute(value, axis, [(i, i ^ mask) for i in range(lax.axis_size(axi...  20.4 us
    all_to_all x2, starting transfers between devices, spread(): lax.all_to_all(jnp.broadcast_to(value[None], (n,) + value.shape), axis, 0...  18.2 us
    all_to_all x1, starting transfers between devices, shards(): got = lax.all_to_all(send, COL, 0, 0, tiled=True)  12.3 us
    ppermute x3, waiting for transfers between devices, shards(): lax.ppermute(right_new, 'zl', [(i, (i + r) % nz) for i in range(nz)])  10.5 us
    ppermute x3, starting transfers between devices, shards(): lax.ppermute(right_new, 'zl', [(i, (i + r) % nz) for i in range(nz)])  9.2 us
    all_to_all x1, waiting for transfers between devices, shards(): lax.all_to_all(both, 'x', 0, 0, tiled=True).astype(F32)  9.05 us
  transfers between devices with their start and end apart: 15, of which 11 were waited for; matrix products, arithmetic and copies ran while one was open for 6% of the time, Pallas kernels for 2%

commit v1 on v0

--- a/solution.py
+++ b/solution.py
@@ -20,8 +20,14 @@
     return lax.ppermute(value, axis, [(i, i ^ mask) for i in range(lax.axis_size(axis))])
 
 
-def spread(value, axis, n):
-    return lax.all_to_all(jnp.broadcast_to(value[None], (n,) + value.shape), axis, 0, 0, tiled=True)
+def exchange(value, nz, ny):
+    n = nz * ny
+    groups = [list(range(n)), list(range(2 * n - 1, n - 1, -1))]
+    return lax.all_to_all(value, ("core",) + COL, 0, 0, axis_index_groups=groups, tiled=True)
+
+
+def spread(value, n, nz, ny):
+    return exchange(jnp.broadcast_to(value[None], (n,) + value.shape), nz, ny)
 
 
 VMEM = pl.BlockSpec(memory_space=pltpu.VMEM)
@@ -96,12 +102,16 @@
     rows = width // ncol
     left_stack = left.reshape(NB, kblocks, NB).transpose(1, 0, 2).reshape(ncol, rows, NB)
     send = jnp.stack([left_stack, upper_own.reshape(ncol, rows, NB)], axis=1)
-    got = lax.all_to_all(send, COL, 0, 0, tiled=True)
-    picked = [lax.dynamic_index_in_dim(got[:, 0], sep_blocks[k], 0) for k in range(levels)]
-    picked += [lax.dynamic_index_in_dim(got[:, 1], pos_blocks[k], 0) for k in range(levels)]
+    got = exchange(send, nz, ny)
+
+    def place(member):
+        return jnp.where(core == 1, ncol - 1 - member, member)
+
+    picked = [lax.dynamic_index_in_dim(got[:, 0], place(sep_blocks[k]), 0) for k in range(levels)]
+    picked += [lax.dynamic_index_in_dim(got[:, 1], place(pos_blocks[k]), 0) for k in range(levels)]
     picked = jnp.concatenate(picked, 0)
     picked, left_late = lax.optimization_barrier((picked, left))
-    parts = spread(picked, COL, ncol).transpose(1, 0, 2, 3).reshape(2 * levels, width, NB)
+    parts = spread(picked, ncol, nz, ny).transpose(1, 0, 2, 3).reshape(2 * levels, width, NB)
     left_moved = lax.ppermute(
         left_late, COL, [(a * ny + b, (b // 2) * ny + 2 * a + b % 2) for a in range(nz) for b in range(ny)]
     )
@@ -116,14 +126,23 @@
     )(flags, row_flags[sep_blocks], parts, diag_inverse[0], upper_own)
 
     state, left_moved = lax.optimization_barrier((state, left_moved))
-    left_tile = spread(left_moved, "y", ny)
+    copies = jnp.broadcast_to(left_moved[None], (ny,) + left_moved.shape)
+    left_tile = lax.all_to_all(copies, "y", 0, 0, tiled=True)
     panels, fills = [], []
     axes = (("core", 1), ("zh", 1), ("x", 1), ("x", 2))
     for k in range(levels):
         if k == levels - 1:
             state = state[:, NB:]
         axis, mask = axes[k]
-        other = swap(state, axis, mask)
+        if axis == "zh":
+            part = state.shape[0] // 2
+            crossed = swap(lax.dynamic_slice_in_dim(state, core * part, part, 0), axis, mask)
+        else:
+            other = swap(state, axis, mask)
+        if axis == "zh":
+            shared = swap(crossed, "core", 1)
+            first = core == 0
+            other = jnp.concatenate([jnp.where(first, crossed, shared), jnp.where(first, shared, crossed)], axis=0)
         total = state.astype(F32) + other.astype(F32)
         skip = NB if k < levels - 1 else 0
         fill = dot(pivot_inverse[k], total[:NB, skip:].astype(BF16)).astype(BF16)
@@ -139,14 +158,14 @@
     fill_own = jnp.concatenate([f[:, -NB:] for f in fills], axis=0)
     right_new = (right_own.astype(F32) - dot(jnp.concatenate(panels, axis=1), fill_own)).astype(BF16)
     right_parts = [right_new] + [
-        lax.ppermute(right_new, "zl", [(i, (i + r) % nz) for i in range(nz)]) for r in range(1, nz)
+        swap(right_new, "zl", r) for r in range(1, nz)
     ]
 
     tile_rows = jnp.arange(nz, dtype=jnp.int32)[:, None] * 8 + 2 * zl + jnp.arange(2, dtype=jnp.int32)[None, :]
     tile_flags = -row_flags[tile_rows.reshape(-1)]
 
     def product(which, dtype):
-        picks = (zl - 2 * which - jnp.arange(2, dtype=jnp.int32)) % nz
+        picks = zl ^ (2 * which + jnp.arange(2, dtype=jnp.int32))
         specs = [SMEM] * 2 + [VMEM] * (1 + nz)
         scratch = [pltpu.VMEM((nz, width, NB), BF16)]
         return call(product_kernel, [(ny * NB, half)], specs, scratch, dtype)(picks, tile_flags, left_tile, *right_parts)[0]

time: 204 us -> 196 us (0.961)
  the two profiles are of different devices: /device:TPU:64 before, /device:TPU:137 now
where the time goes in v1:
time: 196 us; the launch traced here: 195 us
  starting transfers between devices  86.2 us (44%)
  waiting for transfers between devices  73.5 us (38%)
  local copies, waits for them, and re-layouts  11.1 us (6%)
  between operations  10.6 us (5%)
  other arithmetic  6.68 us (3%)
  Pallas kernels  4.65 us (2%)
  matrix products  2.35 us (1%)
    ppermute x9, starting transfers between devices, swap(): lax.ppermute(value, axis, [(i, i ^ mask) for i in range(lax.axis_size(axi...  35.5 us
    ppermute x9, waiting for transfers between devices, swap(): lax.ppermute(value, axis, [(i, i ^ mask) for i in range(lax.axis_size(axi...  30 us
    all_to_all x2, waiting for transfers between devices, exchange(): lax.all_to_all(value, ('core',) + COL, 0, 0, axis_index_groups=groups, ti...  24.6 us
    all_to_all x2, starting transfers between devices, exchange(): lax.all_to_all(value, ('core',) + COL, 0, 0, axis_index_groups=groups, ti...  18.7 us
    all_to_all x1, starting transfers between devices, shards(): left_tile = lax.all_to_all(copies, 'y', 0, 0, tiled=True)  11.8 us
    ppermute x1, starting transfers between devices, shards(): first = lax.ppermute(first, ('zh', 'core', 'zl'), pairs[0])  8.48 us
    all_to_all x1, waiting for transfers between devices, shards(): lax.all_to_all(both, 'x', 0, 0, tiled=True).astype(F32)  8.19 us
    ppermute x1, starting transfers between devices, shards(): lax.ppermute(left_late, COL, [(a * ny + b, b // 2 * ny + 2 * a + b % 2) f...  5.83 us
  transfers between devices with their start and end apart: 16, of which 11 were waited for; matrix products, arithmetic and copies ran while one was open for 6% of the time, Pallas kernels for 2%

profile of v1, /device:TPU:137, one launch (start us, length us, event | category | flops | bytes accessed | tf_op | source)
XLA Modules:
  0.0 195.0 jit_solution(18245390847168352902)
XLA Ops:
  0.0 1.1 copy.26
  1.3 1.0 pad_maximum_fusion
  2.3 0.8 copy.28
  3.1 9.0 %all-to-all-start = ((bf16[32,2,24,128]{3,2,1,0:T(8,128)(2,1)}), bf16[32,2,24,128]{3,2,1,0:T(8,128)(2,1)S(1)}, u32[]{:S(2)}, u32[]{:S(2)}) async-start(bf16[32,2,24,128]{3,2,1,0:T(8,128)(2,1)} %copy.28), calls=%async_computation | async-start | bytes 786432 | tf_op jit(solution)/shard_map/all_to_all | solution.py:26
  12.1 0.7 fusion.73
  17.9 0.6 fusion.72
  23.8 1.5 broadcast_in_dim.30
  25.3 9.7 %all-to-all-start.1 = ((bf16[32,8,24,128]{3,2,1,0:T(8,128)(2,1)}), bf16[32,8,24,128]{3,2,1,0:T(8,128)(2,1)S(1)}, u32[]{:S(2)}, u32[]{:S(2)}) async-start(bf16[32,8,24,128]{3,2,1,0:T(8,128)(2,1)} %broadcast_in_dim.30), calls=%async_computation.1 | async-start | bytes 3145728 | tf_op jit(solution)/shard_map/all_to_all | solution.py:26
  35.1 0.6 constant_dynamic-slice_fusion.3
  35.7 0.6 gather_fusion.1
  36.3 5.8 %collective-permute-start = (bf16[128,768]{1,0:T(8,128)(2,1)}, bf16[128,768]{1,0:T(8,128)(2,1)S(1)}, u32[]{:S(2)}, u32[]{:S(2)}) collective-permute-start(bf16[128,768]{1,0:T(8,128)(2,1)} %bitcast.26), channel_id=1, source_target_pairs={{0,0},{1,1},{2,8},{3,9},{4,16},{5,17},{6,24},{7,25},{8,2},{9,3},{1... | collective-permute-start | bytes 589832 | tf_op jit(solution)/shard_map/ppermute | solution.py:115
  42.2 0.6 gather_fusion.2
  42.8 0.7 pad_maximum_fusion.1.col_ref
  43.5 24.6 %all-to-all-done.1 = bf16[32,8,24,128]{3,2,1,0:T(8,128)(2,1)S(1)} async-done(((bf16[32,8,24,128]{3,2,1,0:T(8,128)(2,1)}), bf16[32,8,24,128]{3,2,1,0:T(8,128)(2,1)S(1)}, u32[]{:S(2)}, u32[]{:S(2)}) %all-to-all-start.1) | async-done | bytes 1572896 | tf_op jit(solution)/shard_map/all_to_all | solution.py:26
  68.4 1.0 copy-done
  69.4 2.3 %shard_map.73 = (bf16[768,512]{1,0:T(8,128)(2,1)S(1)}, bf16[768,128]{1,0:T(8,128)(2,1)S(1)}, bf16[512,640]{1,0:T(8,128)(2,1)S(1)}) custom-call(f32[5]{0:T(128)S(1)} %pad_maximum_fusion.1.col_ref, f32[4]{0:T(128)S(1)} %gather_fusion.2, bf16[8,768,128]{2,1,0:T(8,128)(2,1)S(1)} %bitcast.66, bf16[1,768,768]{2,1,0:T(8,128)(2,1)S(1)} %bitcast.67, ...), custom_call_target="tpu_custom_call" | custom-call | tf_op jit(solution)/shard_map/pallas_call | solution.py:121
  71.7 5.3 %collective-permute-done = bf16[128,768]{1,0:T(8,128)(2,1)S(1)} collective-permute-done((bf16[128,768]{1,0:T(8,128)(2,1)}, bf16[128,768]{1,0:T(8,128)(2,1)S(1)}, u32[]{:S(2)}, u32[]{:S(2)}) %collective-permute-start) | collective-permute-done | bytes 196640 | tf_op jit(solution)/shard_map/ppermute | solution.py:115
  77.0 4.5 %collective-permute-start.1 = (bf16[512,640]{1,0:T(8,128)(2,1)S(1)}, bf16[512,640]{1,0:T(8,128)(2,1)}, u32[]{:S(2)}, u32[]{:S(2)}) collective-permute-start(bf16[512,640]{1,0:T(8,128)(2,1)S(1)} %get-tuple-element.18), channel_id=1, source_target_pairs={{0,32},{32,0},{1,33},{33,1},{2,34},{34,2},{3,35},{35,3},{4,36},{36... | collective-permute-start | bytes 1966088 | tf_op jit(solution)/shard_map/ppermute | solution.py:20
  81.7 0.7 slice.141
  82.4 1.3 broadcast_in_dim.54
  83.7 11.8 %all-to-all-start.2 = ((bf16[8,128,768]{2,1,0:T(8,128)(2,1)}), bf16[8,128,768]{2,1,0:T(8,128)(2,1)S(1)}, u32[]{:S(2)}, u32[]{:S(2)}) async-start(bf16[8,128,768]{2,1,0:T(8,128)(2,1)} %broadcast_in_dim.54), calls=%async_computation.2 | async-start | bytes 3145728 | tf_op jit(solution)/shard_map/all_to_all | solution.py:130
  95.6 1.3 convert_add_fusion
  97.3 7.9 %collective-permute-start.2 = (bf16[192,512]{1,0:T(8,128)(2,1)S(1)}, bf16[192,512]{1,0:T(8,128)(2,1)S(1)}, u32[]{:S(2)}, u32[]{:S(2)}) collective-permute-start(bf16[192,512]{1,0:T(8,128)(2,1)S(1)} %constant_dynamic-slice_fusion.2), channel_id=1, source_target_pairs={{0,64},{64,0},{1,65},{65,1},{2,66},{66,2},{3,67},{67,3},{4,68},{68... | collective-permute-start | bytes 589832 | tf_op jit(solution)/shard_map/ppermute | solution.py:20
  105.5 8.7 %collective-permute-done.2 = bf16[192,512]{1,0:T(8,128)(2,1)S(1)} collective-permute-done((bf16[192,512]{1,0:T(8,128)(2,1)S(1)}, bf16[192,512]{1,0:T(8,128)(2,1)S(1)}, u32[]{:S(2)}, u32[]{:S(2)}) %collective-permute-start.2) | collective-permute-done | bytes 196640 | tf_op jit(solution)/shard_map/ppermute | solution.py:20
  114.2 3.2 %collective-permute-start.3 = (bf16[192,512]{1,0:T(8,128)(2,1)S(1)}, bf16[192,512]{1,0:T(8,128)(2,1)S(1)}, u32[]{:S(2)}, u32[]{:S(2)}) collective-permute-start(bf16[192,512]{1,0:T(8,128)(2,1)S(1)} %collective-permute-done.2), channel_id=1, source_target_pairs={{0,32},{32,0},{1,33},{33,1},{2,34},{34,2},{3,35},{35,3},{4,36},{36... | collective-permute-start | bytes 589832 | tf_op jit(solution)/shard_map/ppermute | solution.py:20
  117.4 1.0 collective-permute-done.3
  119.0 3.1 %collective-permute-start.4 = (bf16[256,384]{1,0:T(8,128)(2,1)S(1)}, bf16[256,384]{1,0:T(8,128)(2,1)S(1)}, u32[]{:S(2)}, u32[]{:S(2)}) collective-permute-start(bf16[256,384]{1,0:T(8,128)(2,1)S(1)} %fusion.3), channel_id=1, source_target_pairs={{0,128},{128,0},{256,384},{384,256},{1,129},{129,1},{257,385},{385... | collective-permute-start | bytes 589832 | tf_op jit(solution)/shard_map/ppermute | solution.py:20
  122.4 4.6 %collective-permute-done.4 = bf16[256,384]{1,0:T(8,128)(2,1)S(1)} collective-permute-done((bf16[256,384]{1,0:T(8,128)(2,1)S(1)}, bf16[256,384]{1,0:T(8,128)(2,1)S(1)}, u32[]{:S(2)}, u32[]{:S(2)}) %collective-permute-start.4) | collective-permute-done | bytes 196640 | tf_op jit(solution)/shard_map/ppermute | solution.py:20
  127.4 4.6 %collective-permute-start.5 = (bf16[128,128]{1,0:T(8,128)(2,1)S(1)}, bf16[128,128]{1,0:T(8,128)(2,1)S(1)}, u32[]{:S(2)}, u32[]{:S(2)}) collective-permute-start(bf16[128,128]{1,0:T(8,128)(2,1)S(1)} %fusion.40), channel_id=1, source_target_pairs={{0,256},{128,384},{256,0},{384,128},{1,257},{129,385},{257,1},{385... | collective-permute-start | bytes 98312 | tf_op jit(solution)/shard_map/ppermute | solution.py:20
  132.4 1.5 collective-permute-done.5
  134.4 1.9 collective-permute-start.6
  136.3 3.7 %collective-permute-start.7 = (bf16[768,128]{1,0:T(8,128)(2,1)S(1)}, bf16[768,128]{1,0:T(8,128)(2,1)S(1)}, u32[]{:S(2)}, u32[]{:S(2)}) collective-permute-start(bf16[768,128]{1,0:T(8,128)(2,1)S(1)} %fusion.refs_0_), channel_id=1, source_target_pairs={{0,16},{8,24},{16,0},{24,8},{1,17},{9,25},{17,1},{25,9},{2,18},{10... | collective-permute-start | bytes 589832 | tf_op jit(solution)/shard_map/ppermute | solution.py:20
  140.0 2.7 %collective-permute-start.8 = (bf16[768,128]{1,0:T(8,128)(2,1)S(1)}, bf16[768,128]{1,0:T(8,128)(2,1)S(1)}, u32[]{:S(2)}, u32[]{:S(2)}) collective-permute-start(bf16[768,128]{1,0:T(8,128)(2,1)S(1)} %fusion.refs_0_), channel_id=1, source_target_pairs={{0,24},{8,16},{16,8},{24,0},{1,25},{9,17},{17,9},{25,1},{2,26},{10... | collective-permute-start | bytes 589832 | tf_op jit(solution)/shard_map/ppermute | solution.py:20
  142.8 0.6 gather_fusion
  143.4 7.9 %collective-permute-done.7.refs_2_ = bf16[768,128]{1,0:T(8,128)(2,1)S(1)} collective-permute-done((bf16[768,128]{1,0:T(8,128)(2,1)S(1)}, bf16[768,128]{1,0:T(8,128)(2,1)S(1)}, u32[]{:S(2)}, u32[]{:S(2)}) %collective-permute-start.7) | collective-permute-done | bytes 196640 | tf_op jit(solution)/shard_map/ppermute | solution.py:20
  151.3 6.0 %collective-permute-done.8.refs_3_ = bf16[768,128]{1,0:T(8,128)(2,1)S(1)} collective-permute-done((bf16[768,128]{1,0:T(8,128)(2,1)S(1)}, bf16[768,128]{1,0:T(8,128)(2,1)S(1)}, u32[]{:S(2)}, u32[]{:S(2)}) %collective-permute-start.8) | collective-permute-done | bytes 196640 | tf_op jit(solution)/shard_map/ppermute | solution.py:20
  157.3 1.2 shard_map.75
  158.5 3.7 %collective-permute-start.9 = (bf16[1024,256]{1,0:T(8,128)(2,1)S(1)}, bf16[1024,256]{1,0:T(8,128)(2,1)S(1)}, u32[]{:S(2)}, u32[]{:S(2)}) collective-permute-start(bf16[1024,256]{1,0:T(8,128)(2,1)S(1)} %shard_map.75), channel_id=1, source_target_pairs={{0,32},{32,0},{1,33},{33,1},{2,34},{34,2},{3,35},{35,3},{4,36},{36... | collective-permute-start | bytes 1572872 | tf_op jit(solution)/shard_map/ppermute | solution.py:20
  162.3 1.2 shard_map.74
  163.8 1.0 add_convert_fusion
  164.7 4.0 %all-to-all-start.3 = ((bf16[4,256,256]{2,1,0:T(8,128)(2,1)}), bf16[4,256,256]{2,1,0:T(8,128)(2,1)S(1)}, u32[]{:S(2)}, u32[]{:S(2)}) async-start(bf16[4,256,256]{2,1,0:T(8,128)(2,1)} %bitcast.39), calls=%async_computation.3 | async-start | bytes 1048576 | tf_op jit(solution)/shard_map/all_to_all | solution.py:175
  168.7 0.6 compare_reduce_fusion.1
  169.5 8.2 %all-to-all-done.3 = bf16[4,256,256]{2,1,0:T(8,128)(2,1)S(1)} async-done(((bf16[4,256,256]{2,1,0:T(8,128)(2,1)}), bf16[4,256,256]{2,1,0:T(8,128)(2,1)S(1)}, u32[]{:S(2)}, u32[]{:S(2)}) %all-to-all-start.3) | async-done | bytes 524320 | tf_op jit(solution)/shard_map/all_to_all | solution.py:175
  177.8 8.5 %collective-permute-start.10 = (bf16[256,128]{1,0:T(8,128)(2,1)S(1)}, bf16[256,128]{1,0:T(8,128)(2,1)S(1)}, u32[]{:S(2)}, u32[]{:S(2)}) collective-permute-start(bf16[256,128]{1,0:T(8,128)(2,1)S(1)} %get-tuple-element.29), channel_id=1, source_target_pairs={{0,0},{8,32},{16,64},{24,96},{32,16},{40,48},{48,80},{56,112},{64,... | collective-permute-start | bytes 196616 | tf_op jit(solution)/shard_map/ppermute | solution.py:183
  186.2 1.9 collective-permute-start.11
  188.2 0.7 broadcast_and_fusion
  188.8 5.4 %collective-permute-done.11 = bf16[256,128]{1,0:T(8,128)(2,1)S(1)} collective-permute-done((bf16[256,128]{1,0:T(8,128)(2,1)S(1)}, bf16[256,128]{1,0:T(8,128)(2,1)S(1)}, u32[]{:S(2)}, u32[]{:S(2)}) %collective-permute-start.11) | collective-permute-done | bytes 65568 | tf_op jit(solution)/shard_map/ppermute | solution.py:184
  194.3 0.7 select_convert_fusion
  (68 shorter events, 4.2 us)
Async XLA Ops:
  0.0 12.0 %copy-start.4 = (s32[4]{0:T(128)S(1)}, s32[4]{0:T(128)}, u32[]{:S(2)}) copy-start(s32[4]{0:T(128)} %param.13) | copy-start | bytes 52
  0.0 17.7 %copy-start.6 = (s32[32]{0:T(128)S(1)}, s32[32]{0:T(128)}, u32[]{:S(2)}) copy-start(s32[32]{0:T(128)} %param.12) | copy-start | bytes 388
  3.1 20.5 %all-to-all-start = ((bf16[32,2,24,128]{3,2,1,0:T(8,128)(2,1)}), bf16[32,2,24,128]{3,2,1,0:T(8,128)(2,1)S(1)}, u32[]{:S(2)}, u32[]{:S(2)}) async-start(bf16[32,2,24,128]{3,2,1,0:T(8,128)(2,1)} %copy.28), calls=%async_computation | async-start | bytes 786432 | tf_op jit(solution)/shard_map/all_to_all | solution.py:26
  25.3 9.7 %copy-start.5 = (s32[1,2,32]{2,1,0:T(2,128)S(1)}, s32[1,2,32]{2,1,0:T(2,128)}, u32[]{:S(2)}) copy-start(s32[1,2,32]{2,1,0:T(2,128)} %param.11) | copy-start | bytes 772
  25.3 42.8 %all-to-all-start.1 = ((bf16[32,8,24,128]{3,2,1,0:T(8,128)(2,1)}), bf16[32,8,24,128]{3,2,1,0:T(8,128)(2,1)S(1)}, u32[]{:S(2)}, u32[]{:S(2)}) async-start(bf16[32,8,24,128]{3,2,1,0:T(8,128)(2,1)} %broadcast_in_dim.30), calls=%async_computation.1 | async-start | bytes 3145728 | tf_op jit(solution)/shard_map/all_to_all | solution.py:26
  36.3 40.7 %collective-permute-start = (bf16[128,768]{1,0:T(8,128)(2,1)}, bf16[128,768]{1,0:T(8,128)(2,1)S(1)}, u32[]{:S(2)}, u32[]{:S(2)}) collective-permute-start(bf16[128,768]{1,0:T(8,128)(2,1)} %bitcast.26), channel_id=1, source_target_pairs={{0,0},{1,1},{2,8},{3,9},{4,16},{5,17},{6,24},{7,25},{8,2},{9,3},{1... | collective-permute-start | bytes 589832 | tf_op jit(solution)/shard_map/ppermute | solution.py:115
  68.2 1.3 copy-start
  68.2 1.3 copy-start.1
  77.0 18.5 %collective-permute-start.1 = (bf16[512,640]{1,0:T(8,128)(2,1)S(1)}, bf16[512,640]{1,0:T(8,128)(2,1)}, u32[]{:S(2)}, u32[]{:S(2)}) collective-permute-start(bf16[512,640]{1,0:T(8,128)(2,1)S(1)} %get-tuple-element.18), channel_id=1, source_target_pairs={{0,32},{32,0},{1,33},{33,1},{2,34},{34,2},{3,35},{35,3},{4,36},{36... | collective-permute-start | bytes 1966088 | tf_op jit(solution)/shard_map/ppermute | solution.py:20
  83.7 73.6 %all-to-all-start.2 = ((bf16[8,128,768]{2,1,0:T(8,128)(2,1)}), bf16[8,128,768]{2,1,0:T(8,128)(2,1)S(1)}, u32[]{:S(2)}, u32[]{:S(2)}) async-start(bf16[8,128,768]{2,1,0:T(8,128)(2,1)} %broadcast_in_dim.54), calls=%async_computation.2 | async-start | bytes 3145728 | tf_op jit(solution)/shard_map/all_to_all | solution.py:130
  95.6 1.3 copy-start.3
  97.3 16.9 %collective-permute-start.2 = (bf16[192,512]{1,0:T(8,128)(2,1)S(1)}, bf16[192,512]{1,0:T(8,128)(2,1)S(1)}, u32[]{:S(2)}, u32[]{:S(2)}) collective-permute-start(bf16[192,512]{1,0:T(8,128)(2,1)S(1)} %constant_dynamic-slice_fusion.2), channel_id=1, source_target_pairs={{0,64},{64,0},{1,65},{65,1},{2,66},{66,2},{3,67},{67,3},{4,68},{68... | collective-permute-start | bytes 589832 | tf_op jit(solution)/shard_map/ppermute | solution.py:20
  114.2 4.3 %collective-permute-start.3 = (bf16[192,512]{1,0:T(8,128)(2,1)S(1)}, bf16[192,512]{1,0:T(8,128)(2,1)S(1)}, u32[]{:S(2)}, u32[]{:S(2)}) collective-permute-start(bf16[192,512]{1,0:T(8,128)(2,1)S(1)} %collective-permute-done.2), channel_id=1, source_target_pairs={{0,32},{32,0},{1,33},{33,1},{2,34},{34,2},{3,35},{35,3},{4,36},{36... | collective-permute-start | bytes 589832 | tf_op jit(solution)/shard_map/ppermute | solution.py:20
  118.5 3.7 %copy-start.2 = (bf16[768,128]{1,0:T(8,128)(2,1)S(1)}, bf16[768,128]{1,0:T(8,128)(2,1)}, u32[]{:S(2)}) copy-start(bf16[768,128]{1,0:T(8,128)(2,1)} %slice.141) | copy-start | bytes 589828
  119.0 8.0 %collective-permute-start.4 = (bf16[256,384]{1,0:T(8,128)(2,1)S(1)}, bf16[256,384]{1,0:T(8,128)(2,1)S(1)}, u32[]{:S(2)}, u32[]{:S(2)}) collective-permute-start(bf16[256,384]{1,0:T(8,128)(2,1)S(1)} %fusion.3), channel_id=1, source_target_pairs={{0,128},{128,0},{256,384},{384,256},{1,129},{129,1},{257,385},{385... | collective-permute-start | bytes 589832 | tf_op jit(solution)/shard_map/ppermute | solution.py:20
  127.4 6.5 %collective-permute-start.5 = (bf16[128,128]{1,0:T(8,128)(2,1)S(1)}, bf16[128,128]{1,0:T(8,128)(2,1)S(1)}, u32[]{:S(2)}, u32[]{:S(2)}) collective-permute-start(bf16[128,128]{1,0:T(8,128)(2,1)S(1)} %fusion.40), channel_id=1, source_target_pairs={{0,256},{128,384},{256,0},{384,128},{1,257},{129,385},{257,1},{385... | collective-permute-start | bytes 98312 | tf_op jit(solution)/shard_map/ppermute | solution.py:20
  134.4 9.1 %collective-permute-start.6 = (bf16[768,128]{1,0:T(8,128)(2,1)S(1)}, bf16[768,128]{1,0:T(8,128)(2,1)S(1)}, u32[]{:S(2)}, u32[]{:S(2)}) collective-permute-start(bf16[768,128]{1,0:T(8,128)(2,1)S(1)} %fusion.refs_0_), channel_id=1, source_target_pairs={{0,8},{8,0},{16,24},{24,16},{1,9},{9,1},{17,25},{25,17},{2,10},{10... | collective-permute-start | bytes 589832 | tf_op jit(solution)/shard_map/ppermute | solution.py:20
  136.3 15.1 %collective-permute-start.7 = (bf16[768,128]{1,0:T(8,128)(2,1)S(1)}, bf16[768,128]{1,0:T(8,128)(2,1)S(1)}, u32[]{:S(2)}, u32[]{:S(2)}) collective-permute-start(bf16[768,128]{1,0:T(8,128)(2,1)S(1)} %fusion.refs_0_), channel_id=1, source_target_pairs={{0,16},{8,24},{16,0},{24,8},{1,17},{9,25},{17,1},{25,9},{2,18},{10... | collective-permute-start | bytes 589832 | tf_op jit(solution)/shard_map/ppermute | solution.py:20
  140.0 17.3 %collective-permute-start.8 = (bf16[768,128]{1,0:T(8,128)(2,1)S(1)}, bf16[768,128]{1,0:T(8,128)(2,1)S(1)}, u32[]{:S(2)}, u32[]{:S(2)}) collective-permute-start(bf16[768,128]{1,0:T(8,128)(2,1)S(1)} %fusion.refs_0_), channel_id=1, source_target_pairs={{0,24},{8,16},{16,8},{24,0},{1,25},{9,17},{17,9},{25,1},{2,26},{10... | collective-permute-start | bytes 589832 | tf_op jit(solution)/shard_map/ppermute | solution.py:20
  158.5 5.2 %collective-permute-start.9 = (bf16[1024,256]{1,0:T(8,128)(2,1)S(1)}, bf16[1024,256]{1,0:T(8,128)(2,1)S(1)}, u32[]{:S(2)}, u32[]{:S(2)}) collective-permute-start(bf16[1024,256]{1,0:T(8,128)(2,1)S(1)} %shard_map.75), channel_id=1, source_target_pairs={{0,32},{32,0},{1,33},{33,1},{2,34},{34,2},{3,35},{35,3},{4,36},{36... | collective-permute-start | bytes 1572872 | tf_op jit(solution)/shard_map/ppermute | solution.py:20
  164.7 12.9 %all-to-all-start.3 = ((bf16[4,256,256]{2,1,0:T(8,128)(2,1)}), bf16[4,256,256]{2,1,0:T(8,128)(2,1)S(1)}, u32[]{:S(2)}, u32[]{:S(2)}) async-start(bf16[4,256,256]{2,1,0:T(8,128)(2,1)} %bitcast.39), calls=%async_computation.3 | async-start | bytes 1048576 | tf_op jit(solution)/shard_map/all_to_all | solution.py:175
  177.8 11.1 %collective-permute-start.10 = (bf16[256,128]{1,0:T(8,128)(2,1)S(1)}, bf16[256,128]{1,0:T(8,128)(2,1)S(1)}, u32[]{:S(2)}, u32[]{:S(2)}) collective-permute-start(bf16[256,128]{1,0:T(8,128)(2,1)S(1)} %get-tuple-element.29), channel_id=1, source_target_pairs={{0,0},{8,32},{16,64},{24,96},{32,16},{40,48},{48,80},{56,112},{64,... | collective-permute-start | bytes 196616 | tf_op jit(solution)/shard_map/ppermute | solution.py:183
  186.2 8.0 %collective-permute-start.11 = (bf16[256,128]{1,0:T(8,128)(2,1)S(1)}, bf16[256,128]{1,0:T(8,128)(2,1)S(1)}, u32[]{:S(2)}, u32[]{:S(2)}) collective-permute-start(bf16[256,128]{1,0:T(8,128)(2,1)S(1)} %get-tuple-element.30), channel_id=1, source_target_pairs={{0,8},{8,40},{16,72},{24,104},{32,24},{40,56},{48,88},{56,120},{64... | collective-permute-start | bytes 196616 | tf_op jit(solution)/shard_map/ppermute | solution.py:184

commit v2 on v1

--- a/solution.py
+++ b/solution.py
@@ -68,7 +68,7 @@
         right_ref[r] = part[...]
     right = jnp.concatenate([right_ref[pick_ref[0]], right_ref[pick_ref[1]]], axis=1)
     for q in range(left_ref.shape[0]):
-        here = pl.ds(q * NB, NB)
+        here = pl.ds(pl.multiple_of(pick_ref[2 + q] * NB, NB), NB)
         out_ref[here, :] = (dot(left_ref[q], right) * flag_ref[q]).astype(out_ref.dtype)
 
 
@@ -127,7 +127,10 @@
 
     state, left_moved = lax.optimization_barrier((state, left_moved))
     copies = jnp.broadcast_to(left_moved[None], (ny,) + left_moved.shape)
-    left_tile = lax.all_to_all(copies, "y", 0, 0, tiled=True)
+    members = [
+        [(c * nz + a) * ny + (b if c == 0 else ny - 1 - b) for b in range(ny)] for c in range(2) for a in range(nz)
+    ]
+    left_tile = lax.all_to_all(copies, ("core",) + COL, 0, 0, axis_index_groups=members, tiled=True)
     panels, fills = [], []
     axes = (("core", 1), ("zh", 1), ("x", 1), ("x", 2))
     for k in range(levels):
@@ -162,10 +165,13 @@
     ]
 
     tile_rows = jnp.arange(nz, dtype=jnp.int32)[:, None] * 8 + 2 * zl + jnp.arange(2, dtype=jnp.int32)[None, :]
-    tile_flags = -row_flags[tile_rows.reshape(-1)]
+    order = jnp.arange(ny, dtype=jnp.int32)
+    order = jnp.where(core == 1, ny - 1 - order, order)
+    tile_flags = -row_flags[tile_rows.reshape(-1)[order]]
 
     def product(which, dtype):
         picks = zl ^ (2 * which + jnp.arange(2, dtype=jnp.int32))
+        picks = jnp.concatenate([picks, order])
         specs = [SMEM] * 2 + [VMEM] * (1 + nz)
         scratch = [pltpu.VMEM((nz, width, NB), BF16)]
         return call(product_kernel, [(ny * NB, half)], specs, scratch, dtype)(picks, tile_flags, left_tile, *right_parts)[0]

time: 196 us -> 197 us (level)
  the two profiles are of different devices: /device:TPU:137 before, /device:TPU:9 now
where the time goes in v2:
time: 197 us; the launch traced here: 196 us
  starting transfers between devices  90.9 us (46%)
  waiting for transfers between devices  69.4 us (35%)
  local copies, waits for them, and re-layouts  11.7 us (6%)
  between operations  10.5 us (5%)
  other arithmetic  6.73 us (3%)
  Pallas kernels  4.64 us (2%)
  matrix products  2.35 us (1%)
    ppermute x9, starting transfers between devices, swap(): lax.ppermute(value, axis, [(i, i ^ mask) for i in range(lax.axis_size(axi...  48.5 us
    all_to_all x2, waiting for transfers between devices, exchange(): lax.all_to_all(value, ('core',) + COL, 0, 0, axis_index_groups=groups, ti...  29.8 us
    ppermute x9, waiting for transfers between devices, swap(): lax.ppermute(value, axis, [(i, i ^ mask) for i in range(lax.axis_size(axi...  25.4 us
    all_to_all x2, starting transfers between devices, exchange(): lax.all_to_all(value, ('core',) + COL, 0, 0, axis_index_groups=groups, ti...  22.4 us
    all_to_all x1, waiting for transfers between devices, shards(): lax.all_to_all(both, 'x', 0, 0, tiled=True).astype(F32)  8.19 us
    ppermute x1, starting transfers between devices, shards(): first = lax.ppermute(first, ('zh', 'core', 'zl'), pairs[0])  6.44 us
    ppermute x1, waiting for transfers between devices, shards(): second = lax.ppermute(second, ('zh', 'core', 'zl'), pairs[1])  6.02 us
    all_to_all x1, starting transfers between devices, shards(): lax.all_to_all(copies, ('core',) + COL, 0, 0, axis_index_groups=members,...  4.95 us
  transfers between devices with their start and end apart: 16, of which 9 were waited for; matrix products, arithmetic and copies ran while one was open for 7% of the time, Pallas kernels for 2%

profile of v2, /device:TPU:9, one launch (start us, length us, event | category | flops | bytes accessed | tf_op | source)
XLA Modules:
  0.0 196.3 jit_solution(17362058021344263838)
XLA Ops:
  0.0 1.1 copy.26
  1.3 1.0 pad_maximum_fusion
  2.3 0.8 copy.28
  3.1 12.7 %all-to-all-start = ((bf16[32,2,24,128]{3,2,1,0:T(8,128)(2,1)}), bf16[32,2,24,128]{3,2,1,0:T(8,128)(2,1)S(1)}, u32[]{:S(2)}, u32[]{:S(2)}) async-start(bf16[32,2,24,128]{3,2,1,0:T(8,128)(2,1)} %copy.28), calls=%async_computation | async-start | bytes 786432 | tf_op jit(solution)/shard_map/all_to_all | solution.py:26
  15.7 0.7 fusion.74
  21.6 0.7 fusion.73
  27.5 1.5 broadcast_in_dim.30
  29.0 9.7 %all-to-all-start.1 = ((bf16[32,8,24,128]{3,2,1,0:T(8,128)(2,1)}), bf16[32,8,24,128]{3,2,1,0:T(8,128)(2,1)S(1)}, u32[]{:S(2)}, u32[]{:S(2)}) async-start(bf16[32,8,24,128]{3,2,1,0:T(8,128)(2,1)} %broadcast_in_dim.30), calls=%async_computation.1 | async-start | bytes 3145728 | tf_op jit(solution)/shard_map/all_to_all | solution.py:26
  38.9 0.6 constant_dynamic-slice_fusion.3
  39.5 0.6 gather_fusion.2
  40.2 0.6 gather_fusion.3
  40.8 1.6 collective-permute-start
  42.4 0.7 pad_maximum_fusion.1.col_ref
  43.1 29.8 %all-to-all-done.1 = bf16[32,8,24,128]{3,2,1,0:T(8,128)(2,1)S(1)} async-done(((bf16[32,8,24,128]{3,2,1,0:T(8,128)(2,1)}), bf16[32,8,24,128]{3,2,1,0:T(8,128)(2,1)S(1)}, u32[]{:S(2)}, u32[]{:S(2)}) %all-to-all-start.1) | async-done | bytes 1572896 | tf_op jit(solution)/shard_map/all_to_all | solution.py:26
  73.2 1.0 copy-done
  74.2 2.3 %shard_map.73 = (bf16[768,512]{1,0:T(8,128)(2,1)S(1)}, bf16[768,128]{1,0:T(8,128)(2,1)S(1)}, bf16[512,640]{1,0:T(8,128)(2,1)S(1)}) custom-call(f32[5]{0:T(128)S(1)} %pad_maximum_fusion.1.col_ref, f32[4]{0:T(128)S(1)} %gather_fusion.3, bf16[8,768,128]{2,1,0:T(8,128)(2,1)S(1)} %bitcast.70, bf16[1,768,768]{2,1,0:T(8,128)(2,1)S(1)} %bitcast.71, ...), custom_call_target="tpu_custom_call" | custom-call | tf_op jit(solution)/shard_map/pallas_call | solution.py:121
  76.4 15.7 %collective-permute-start.1 = (bf16[512,640]{1,0:T(8,128)(2,1)S(1)}, bf16[512,640]{1,0:T(8,128)(2,1)}, u32[]{:S(2)}, u32[]{:S(2)}) collective-permute-start(bf16[512,640]{1,0:T(8,128)(2,1)S(1)} %get-tuple-element.18), channel_id=1, source_target_pairs={{0,32},{32,0},{1,33},{33,1},{2,34},{34,2},{3,35},{35,3},{4,36},{36... | collective-permute-start | bytes 1966088 | tf_op jit(solution)/shard_map/ppermute | solution.py:20
  92.2 0.6 gather_fusion
  92.8 0.6 gather_fusion.1
  93.5 0.7 slice.141
  94.2 1.3 broadcast_in_dim.31
  95.5 4.9 %all-to-all-start.2 = ((bf16[8,128,768]{2,1,0:T(8,128)(2,1)}), bf16[8,128,768]{2,1,0:T(8,128)(2,1)S(1)}, u32[]{:S(2)}, u32[]{:S(2)}) async-start(bf16[8,128,768]{2,1,0:T(8,128)(2,1)} %broadcast_in_dim.31), calls=%async_computation.2 | async-start | bytes 3145728 | tf_op jit(solution)/shard_map/all_to_all | solution.py:133
  100.5 1.3 convert_add_fusion
  102.2 7.9 %collective-permute-start.2 = (bf16[192,512]{1,0:T(8,128)(2,1)S(1)}, bf16[192,512]{1,0:T(8,128)(2,1)S(1)}, u32[]{:S(2)}, u32[]{:S(2)}) collective-permute-start(bf16[192,512]{1,0:T(8,128)(2,1)S(1)} %constant_dynamic-slice_fusion.2), channel_id=1, source_target_pairs={{0,64},{64,0},{1,65},{65,1},{2,66},{66,2},{3,67},{67,3},{4,68},{68... | collective-permute-start | bytes 589832 | tf_op jit(solution)/shard_map/ppermute | solution.py:20
  110.4 6.9 %collective-permute-done.2 = bf16[192,512]{1,0:T(8,128)(2,1)S(1)} collective-permute-done((bf16[192,512]{1,0:T(8,128)(2,1)S(1)}, bf16[192,512]{1,0:T(8,128)(2,1)S(1)}, u32[]{:S(2)}, u32[]{:S(2)}) %collective-permute-start.2) | collective-permute-done | bytes 196640 | tf_op jit(solution)/shard_map/ppermute | solution.py:20
  117.3 1.9 collective-permute-start.3
  119.2 1.4 collective-permute-done.3
  121.2 3.1 %collective-permute-start.4 = (bf16[256,384]{1,0:T(8,128)(2,1)S(1)}, bf16[256,384]{1,0:T(8,128)(2,1)S(1)}, u32[]{:S(2)}, u32[]{:S(2)}) collective-permute-start(bf16[256,384]{1,0:T(8,128)(2,1)S(1)} %fusion.3), channel_id=1, source_target_pairs={{0,128},{128,0},{256,384},{384,256},{1,129},{129,1},{257,385},{385... | collective-permute-start | bytes 589832 | tf_op jit(solution)/shard_map/ppermute | solution.py:20
  124.6 4.8 %collective-permute-done.4 = bf16[256,384]{1,0:T(8,128)(2,1)S(1)} collective-permute-done((bf16[256,384]{1,0:T(8,128)(2,1)S(1)}, bf16[256,384]{1,0:T(8,128)(2,1)S(1)}, u32[]{:S(2)}, u32[]{:S(2)}) %collective-permute-start.4) | collective-permute-done | bytes 196640 | tf_op jit(solution)/shard_map/ppermute | solution.py:20
  129.8 4.7 %collective-permute-start.5 = (bf16[128,128]{1,0:T(8,128)(2,1)S(1)}, bf16[128,128]{1,0:T(8,128)(2,1)S(1)}, u32[]{:S(2)}, u32[]{:S(2)}) collective-permute-start(bf16[128,128]{1,0:T(8,128)(2,1)S(1)} %fusion.40), channel_id=1, source_target_pairs={{0,256},{128,384},{256,0},{384,128},{1,257},{129,385},{257,1},{385... | collective-permute-start | bytes 98312 | tf_op jit(solution)/shard_map/ppermute | solution.py:20
  134.8 1.5 collective-permute-done.5
  136.4 0.4 fusion.refs_0_
  136.8 4.2 %collective-permute-start.6 = (bf16[768,128]{1,0:T(8,128)(2,1)S(1)}, bf16[768,128]{1,0:T(8,128)(2,1)S(1)}, u32[]{:S(2)}, u32[]{:S(2)}) collective-permute-start(bf16[768,128]{1,0:T(8,128)(2,1)S(1)} %fusion.refs_0_), channel_id=1, source_target_pairs={{0,8},{8,0},{16,24},{24,16},{1,9},{9,1},{17,25},{25,17},{2,10},{10... | collective-permute-start | bytes 589832 | tf_op jit(solution)/shard_map/ppermute | solution.py:20
  141.0 1.9 collective-permute-start.7
  142.9 4.0 %collective-permute-start.8 = (bf16[768,128]{1,0:T(8,128)(2,1)S(1)}, bf16[768,128]{1,0:T(8,128)(2,1)S(1)}, u32[]{:S(2)}, u32[]{:S(2)}) collective-permute-start(bf16[768,128]{1,0:T(8,128)(2,1)S(1)} %fusion.refs_0_), channel_id=1, source_target_pairs={{0,24},{8,16},{16,8},{24,0},{1,25},{9,17},{17,9},{25,1},{2,26},{10... | collective-permute-start | bytes 589832 | tf_op jit(solution)/shard_map/ppermute | solution.py:20
  147.0 10.6 %collective-permute-done.7.refs_2_ = bf16[768,128]{1,0:T(8,128)(2,1)S(1)} collective-permute-done((bf16[768,128]{1,0:T(8,128)(2,1)S(1)}, bf16[768,128]{1,0:T(8,128)(2,1)S(1)}, u32[]{:S(2)}, u32[]{:S(2)}) %collective-permute-start.7) | collective-permute-done | bytes 196640 | tf_op jit(solution)/shard_map/ppermute | solution.py:20
  157.6 1.2 shard_map.75
  158.7 5.1 %collective-permute-start.9 = (bf16[1024,256]{1,0:T(8,128)(2,1)S(1)}, bf16[1024,256]{1,0:T(8,128)(2,1)S(1)}, u32[]{:S(2)}, u32[]{:S(2)}) collective-permute-start(bf16[1024,256]{1,0:T(8,128)(2,1)S(1)} %shard_map.75), channel_id=1, source_target_pairs={{0,32},{32,0},{1,33},{33,1},{2,34},{34,2},{3,35},{35,3},{4,36},{36... | collective-permute-start | bytes 1572872 | tf_op jit(solution)/shard_map/ppermute | solution.py:20
  163.9 1.2 shard_map.74
  165.4 0.9 add_convert_fusion
  166.3 4.0 %all-to-all-start.3 = ((bf16[4,256,256]{2,1,0:T(8,128)(2,1)}), bf16[4,256,256]{2,1,0:T(8,128)(2,1)S(1)}, u32[]{:S(2)}, u32[]{:S(2)}) async-start(bf16[4,256,256]{2,1,0:T(8,128)(2,1)} %bitcast.41), calls=%async_computation.3 | async-start | bytes 1048576 | tf_op jit(solution)/shard_map/all_to_all | solution.py:181
  170.3 0.6 compare_reduce_fusion.1
  171.1 8.2 %all-to-all-done.3 = bf16[4,256,256]{2,1,0:T(8,128)(2,1)S(1)} async-done(((bf16[4,256,256]{2,1,0:T(8,128)(2,1)}), bf16[4,256,256]{2,1,0:T(8,128)(2,1)S(1)}, u32[]{:S(2)}, u32[]{:S(2)}) %all-to-all-start.3) | async-done | bytes 524320 | tf_op jit(solution)/shard_map/all_to_all | solution.py:181
  179.4 6.4 %collective-permute-start.10 = (bf16[256,128]{1,0:T(8,128)(2,1)S(1)}, bf16[256,128]{1,0:T(8,128)(2,1)S(1)}, u32[]{:S(2)}, u32[]{:S(2)}) collective-permute-start(bf16[256,128]{1,0:T(8,128)(2,1)S(1)} %get-tuple-element.29), channel_id=1, source_target_pairs={{0,0},{8,32},{16,64},{24,96},{32,16},{40,48},{48,80},{56,112},{64,... | collective-permute-start | bytes 196616 | tf_op jit(solution)/shard_map/ppermute | solution.py:189
  185.8 3.1 %collective-permute-start.11 = (bf16[256,128]{1,0:T(8,128)(2,1)S(1)}, bf16[256,128]{1,0:T(8,128)(2,1)S(1)}, u32[]{:S(2)}, u32[]{:S(2)}) collective-permute-start(bf16[256,128]{1,0:T(8,128)(2,1)S(1)} %get-tuple-element.30), channel_id=1, source_target_pairs={{0,8},{8,40},{16,72},{24,104},{32,24},{40,56},{48,88},{56,120},{64... | collective-permute-start | bytes 196616 | tf_op jit(solution)/shard_map/ppermute | solution.py:190
  188.9 0.7 broadcast_and_fusion
  189.5 6.0 %collective-permute-done.11 = bf16[256,128]{1,0:T(8,128)(2,1)S(1)} collective-permute-done((bf16[256,128]{1,0:T(8,128)(2,1)S(1)}, bf16[256,128]{1,0:T(8,128)(2,1)S(1)}, u32[]{:S(2)}, u32[]{:S(2)}) %collective-permute-start.11) | collective-permute-done | bytes 65568 | tf_op jit(solution)/shard_map/ppermute | solution.py:190
  195.6 0.7 select_convert_fusion
  (73 shorter events, 4.0 us)
Async XLA Ops:
  0.0 15.7 %copy-start.4 = (s32[4]{0:T(128)S(1)}, s32[4]{0:T(128)}, u32[]{:S(2)}) copy-start(s32[4]{0:T(128)} %param.13) | copy-start | bytes 52
  0.0 21.4 %copy-start.6 = (s32[32]{0:T(128)S(1)}, s32[32]{0:T(128)}, u32[]{:S(2)}) copy-start(s32[32]{0:T(128)} %param.12) | copy-start | bytes 388
  3.1 24.2 %all-to-all-start = ((bf16[32,2,24,128]{3,2,1,0:T(8,128)(2,1)}), bf16[32,2,24,128]{3,2,1,0:T(8,128)(2,1)S(1)}, u32[]{:S(2)}, u32[]{:S(2)}) async-start(bf16[32,2,24,128]{3,2,1,0:T(8,128)(2,1)} %copy.28), calls=%async_computation | async-start | bytes 786432 | tf_op jit(solution)/shard_map/all_to_all | solution.py:26
  29.0 9.9 %copy-start.5 = (s32[1,2,32]{2,1,0:T(2,128)S(1)}, s32[1,2,32]{2,1,0:T(2,128)}, u32[]{:S(2)}) copy-start(s32[1,2,32]{2,1,0:T(2,128)} %param.11) | copy-start | bytes 772
  29.0 43.9 %all-to-all-start.1 = ((bf16[32,8,24,128]{3,2,1,0:T(8,128)(2,1)}), bf16[32,8,24,128]{3,2,1,0:T(8,128)(2,1)S(1)}, u32[]{:S(2)}, u32[]{:S(2)}) async-start(bf16[32,8,24,128]{3,2,1,0:T(8,128)(2,1)} %broadcast_in_dim.30), calls=%async_computation.1 | async-start | bytes 3145728 | tf_op jit(solution)/shard_map/all_to_all | solution.py:26
  40.8 35.6 %collective-permute-start = (bf16[128,768]{1,0:T(8,128)(2,1)}, bf16[128,768]{1,0:T(8,128)(2,1)S(1)}, u32[]{:S(2)}, u32[]{:S(2)}) collective-permute-start(bf16[128,768]{1,0:T(8,128)(2,1)} %bitcast.28), channel_id=1, source_target_pairs={{0,0},{1,1},{2,8},{3,9},{4,16},{5,17},{6,24},{7,25},{8,2},{9,3},{1... | collective-permute-start | bytes 589832 | tf_op jit(solution)/shard_map/ppermute | solution.py:115
  72.9 1.3 copy-start
  72.9 1.3 copy-start.1
  76.4 24.0 %collective-permute-start.1 = (bf16[512,640]{1,0:T(8,128)(2,1)S(1)}, bf16[512,640]{1,0:T(8,128)(2,1)}, u32[]{:S(2)}, u32[]{:S(2)}) collective-permute-start(bf16[512,640]{1,0:T(8,128)(2,1)S(1)} %get-tuple-element.18), channel_id=1, source_target_pairs={{0,32},{32,0},{1,33},{33,1},{2,34},{34,2},{3,35},{35,3},{4,36},{36... | collective-permute-start | bytes 1966088 | tf_op jit(solution)/shard_map/ppermute | solution.py:20
  95.5 62.0 %all-to-all-start.2 = ((bf16[8,128,768]{2,1,0:T(8,128)(2,1)}), bf16[8,128,768]{2,1,0:T(8,128)(2,1)S(1)}, u32[]{:S(2)}, u32[]{:S(2)}) async-start(bf16[8,128,768]{2,1,0:T(8,128)(2,1)} %broadcast_in_dim.31), calls=%async_computation.2 | async-start | bytes 3145728 | tf_op jit(solution)/shard_map/all_to_all | solution.py:133
  100.5 1.3 copy-start.3
  102.2 15.1 %collective-permute-start.2 = (bf16[192,512]{1,0:T(8,128)(2,1)S(1)}, bf16[192,512]{1,0:T(8,128)(2,1)S(1)}, u32[]{:S(2)}, u32[]{:S(2)}) collective-permute-start(bf16[192,512]{1,0:T(8,128)(2,1)S(1)} %constant_dynamic-slice_fusion.2), channel_id=1, source_target_pairs={{0,64},{64,0},{1,65},{65,1},{2,66},{66,2},{3,67},{67,3},{4,68},{68... | collective-permute-start | bytes 589832 | tf_op jit(solution)/shard_map/ppermute | solution.py:20
  117.3 3.3 %collective-permute-start.3 = (bf16[192,512]{1,0:T(8,128)(2,1)S(1)}, bf16[192,512]{1,0:T(8,128)(2,1)S(1)}, u32[]{:S(2)}, u32[]{:S(2)}) collective-permute-start(bf16[192,512]{1,0:T(8,128)(2,1)S(1)} %collective-permute-done.2), channel_id=1, source_target_pairs={{0,32},{32,0},{1,33},{33,1},{2,34},{34,2},{3,35},{35,3},{4,36},{36... | collective-permute-start | bytes 589832 | tf_op jit(solution)/shard_map/ppermute | solution.py:20
  120.7 3.7 %copy-start.2 = (bf16[768,128]{1,0:T(8,128)(2,1)S(1)}, bf16[768,128]{1,0:T(8,128)(2,1)}, u32[]{:S(2)}) copy-start(bf16[768,128]{1,0:T(8,128)(2,1)} %slice.141) | copy-start | bytes 589828
  121.2 8.2 %collective-permute-start.4 = (bf16[256,384]{1,0:T(8,128)(2,1)S(1)}, bf16[256,384]{1,0:T(8,128)(2,1)S(1)}, u32[]{:S(2)}, u32[]{:S(2)}) collective-permute-start(bf16[256,384]{1,0:T(8,128)(2,1)S(1)} %fusion.3), channel_id=1, source_target_pairs={{0,128},{128,0},{256,384},{384,256},{1,129},{129,1},{257,385},{385... | collective-permute-start | bytes 589832 | tf_op jit(solution)/shard_map/ppermute | solution.py:20
  129.8 6.5 %collective-permute-start.5 = (bf16[128,128]{1,0:T(8,128)(2,1)S(1)}, bf16[128,128]{1,0:T(8,128)(2,1)S(1)}, u32[]{:S(2)}, u32[]{:S(2)}) collective-permute-start(bf16[128,128]{1,0:T(8,128)(2,1)S(1)} %fusion.40), channel_id=1, source_target_pairs={{0,256},{128,384},{256,0},{384,128},{1,257},{129,385},{257,1},{385... | collective-permute-start | bytes 98312 | tf_op jit(solution)/shard_map/ppermute | solution.py:20
  136.8 10.2 %collective-permute-start.6 = (bf16[768,128]{1,0:T(8,128)(2,1)S(1)}, bf16[768,128]{1,0:T(8,128)(2,1)S(1)}, u32[]{:S(2)}, u32[]{:S(2)}) collective-permute-start(bf16[768,128]{1,0:T(8,128)(2,1)S(1)} %fusion.refs_0_), channel_id=1, source_target_pairs={{0,8},{8,0},{16,24},{24,16},{1,9},{9,1},{17,25},{25,17},{2,10},{10... | collective-permute-start | bytes 589832 | tf_op jit(solution)/shard_map/ppermute | solution.py:20
  141.0 16.6 %collective-permute-start.7 = (bf16[768,128]{1,0:T(8,128)(2,1)S(1)}, bf16[768,128]{1,0:T(8,128)(2,1)S(1)}, u32[]{:S(2)}, u32[]{:S(2)}) collective-permute-start(bf16[768,128]{1,0:T(8,128)(2,1)S(1)} %fusion.refs_0_), channel_id=1, source_target_pairs={{0,16},{8,24},{16,0},{24,8},{1,17},{9,25},{17,1},{25,9},{2,18},{10... | collective-permute-start | bytes 589832 | tf_op jit(solution)/shard_map/ppermute | solution.py:20
  142.9 14.7 %collective-permute-start.8 = (bf16[768,128]{1,0:T(8,128)(2,1)S(1)}, bf16[768,128]{1,0:T(8,128)(2,1)S(1)}, u32[]{:S(2)}, u32[]{:S(2)}) collective-permute-start(bf16[768,128]{1,0:T(8,128)(2,1)S(1)} %fusion.refs_0_), channel_id=1, source_target_pairs={{0,24},{8,16},{16,8},{24,0},{1,25},{9,17},{17,9},{25,1},{2,26},{10... | collective-permute-start | bytes 589832 | tf_op jit(solution)/shard_map/ppermute | solution.py:20
  158.7 6.6 %collective-permute-start.9 = (bf16[1024,256]{1,0:T(8,128)(2,1)S(1)}, bf16[1024,256]{1,0:T(8,128)(2,1)S(1)}, u32[]{:S(2)}, u32[]{:S(2)}) collective-permute-start(bf16[1024,256]{1,0:T(8,128)(2,1)S(1)} %shard_map.75), channel_id=1, source_target_pairs={{0,32},{32,0},{1,33},{33,1},{2,34},{34,2},{3,35},{35,3},{4,36},{36... | collective-permute-start | bytes 1572872 | tf_op jit(solution)/shard_map/ppermute | solution.py:20
  166.3 12.9 %all-to-all-start.3 = ((bf16[4,256,256]{2,1,0:T(8,128)(2,1)}), bf16[4,256,256]{2,1,0:T(8,128)(2,1)S(1)}, u32[]{:S(2)}, u32[]{:S(2)}) async-start(bf16[4,256,256]{2,1,0:T(8,128)(2,1)} %bitcast.41), calls=%async_computation.3 | async-start | bytes 1048576 | tf_op jit(solution)/shard_map/all_to_all | solution.py:181
  179.4 10.2 %collective-permute-start.10 = (bf16[256,128]{1,0:T(8,128)(2,1)S(1)}, bf16[256,128]{1,0:T(8,128)(2,1)S(1)}, u32[]{:S(2)}, u32[]{:S(2)}) collective-permute-start(bf16[256,128]{1,0:T(8,128)(2,1)S(1)} %get-tuple-element.29), channel_id=1, source_target_pairs={{0,0},{8,32},{16,64},{24,96},{32,16},{40,48},{48,80},{56,112},{64,... | collective-permute-start | bytes 196616 | tf_op jit(solution)/shard_map/ppermute | solution.py:189
  185.8 9.8 %collective-permute-start.11 = (bf16[256,128]{1,0:T(8,128)(2,1)S(1)}, bf16[256,128]{1,0:T(8,128)(2,1)S(1)}, u32[]{:S(2)}, u32[]{:S(2)}) collective-permute-start(bf16[256,128]{1,0:T(8,128)(2,1)S(1)} %get-tuple-element.30), channel_id=1, source_target_pairs={{0,8},{8,40},{16,72},{24,104},{32,24},{40,56},{48,88},{56,120},{64... | collective-permute-start | bytes 196616 | tf_op jit(solution)/shard_map/ppermute | solution.py:190
